TPU v7x, 128 devices: a whole 4x4x4 slice. The times are simulated.
128 devices in a mesh: song: 16 (over x_lo, z, core), tensor: 8 (over x_hi, y).
Axes of the slice: x: 4 (x_hi: 2, x_lo: 2; x = x_hi * 2 + x_lo), y: 4, z: 4, core: 2. Of those that a mesh axis runs over, the one named last changes fastest.
Arguments:
- upper_codes: int32 [4096], P('song'), may hold values from 0 to 2047
- middle_codes: int32 [16384], P('song'), may hold values from 0 to 2047
- upper_table: bfloat16 [2048, 1024], P(None, 'tensor'), may hold values from -6 to 6
- dilated_weight: bfloat16 [4, 3, 1024, 1024], P(None, None, 'tensor'), may hold values from -0.109375 to 0.109375
- mixing_weight: bfloat16 [4, 1024, 1024], P(None, None, 'tensor'), may hold values from -0.1875 to 0.1875
- upsample_weight: bfloat16 [1024, 7680], P('tensor'), may hold values from -0.1875 to 0.1875
- middle_table: bfloat16 [2048, 1920], P('tensor'), may hold values from -6 to 6
- norm_gain: float32 [1920], replicated, may hold values from 0.1 to 1.9
- qkv_weight: bfloat16 [1920, 16, 384], P(None, 'tensor'), may hold values from -4 to 4
Outputs:
- context: bfloat16 [16384, 2048], P('song', 'tensor')
All inputs are finite; a program needn't handle non-finite values.
Results may differ from a plain program's by a relative error of at most 0.0145.
Values may be sent and summed in bfloat16 or wider, within the bound.
No kernel may reach another device: no remote copies, remote signals or barrier semaphores. Data moves between devices by JAX's collectives and lax.ppermute only.
A program may use at most 128 MiB of HBM per device.

v0:
```python
import jax
import jax.numpy as jnp
from jax import lax
from jax.sharding import PartitionSpec as P

BLOCKS = 4


def extended(cells, sides, width):
    for axis, dim in sides:
        count = lax.axis_size(axis)
        ends = count - 1
        head = lax.slice_in_dim(cells, 0, width, axis=dim)
        tail = lax.slice_in_dim(cells, cells.shape[dim] - width, cells.shape[dim], axis=dim)
        cells = jnp.concatenate(
            [
                lax.ppermute(tail, axis, [(i, (i + 1) % count) for i in range(ends)]),
                cells,
                lax.ppermute(head, axis, [((i + 1) % count, i) for i in range(ends)]),
            ],
            axis=dim,
        )
    return cells


def from_behind(shard, axis, by):
    peers = lax.axis_size(axis)
    pairs = [(i, i + by) for i in range(peers) if 0 <= i + by < peers]
    return lax.ppermute(shard, axis, pairs)


def on_device(
    upper_codes,
    middle_codes,
    upper_table,
    dilated_weight,
    mixing_weight,
    upsample_weight,
    middle_table,
    norm_gain,
    qkv_weight,
):
    tensor_rank = lax.axis_index("tensor")
    song_rank = lax.axis_index("song")
    count = upper_codes.shape[0]
    rows = middle_codes.shape[0]
    width = norm_gain.shape[0]
    upper_vocab = upper_table.shape[0]
    upper_hot = (upper_codes[:, None] == jnp.arange(upper_vocab, dtype=jnp.int32)[None, :]).astype(
        jnp.bfloat16
    )
    state = jnp.dot(upper_hot, upper_table, preferred_element_type=jnp.float32)
    for level in range(BLOCKS):
        step = 3**level
        state_bf = jnp.maximum(state, 0.0).astype(jnp.bfloat16)
        padded = extended(state_bf, (("song", 0),), step)
        partial_value = jnp.dot(
            padded[0:count], dilated_weight[level, 0], preferred_element_type=jnp.float32
        )
        partial_value = partial_value + jnp.dot(
            padded[step : step + count],
            dilated_weight[level, 1],
            preferred_element_type=jnp.float32,
        )
        partial_value = partial_value + jnp.dot(
            padded[2 * step : 2 * step + count],
            dilated_weight[level, 2],
            preferred_element_type=jnp.float32,
        )
        summed = lax.psum(partial_value, "tensor")
        rect = jnp.maximum(summed, 0.0).astype(jnp.bfloat16)
        state = state + jnp.dot(rect, mixing_weight[level], preferred_element_type=jnp.float32)
    final = state.astype(jnp.bfloat16)
    vocab_rows = middle_table.shape[0]
    upsampled = jnp.dot(final, upsample_weight, preferred_element_type=jnp.float32).reshape(
        rows, width
    )
    local_codes = middle_codes - tensor_rank * vocab_rows
    middle_hot = (local_codes[:, None] == jnp.arange(vocab_rows, dtype=jnp.int32)[None, :]).astype(
        jnp.bfloat16
    )
    terms = upsampled + jnp.dot(middle_hot, middle_table, preferred_element_type=jnp.float32)
    frames = lax.psum(terms, "tensor")
    mean = jnp.mean(frames, axis=1, keepdims=True)
    var = jnp.mean((frames - mean) ** 2, axis=1, keepdims=True)
    normed = ((frames - mean) * lax.rsqrt(var + 1e-05) * norm_gain[None, :]).astype(jnp.bfloat16)
    heads_here = qkv_weight.shape[1]
    head_size = qkv_weight.shape[2] // 3
    projected = jnp.dot(
        normed,
        qkv_weight.reshape(width, heads_here * 3 * head_size),
        preferred_element_type=jnp.float32,
    )
    projected = projected.astype(jnp.bfloat16).reshape(rows, heads_here, 3 * head_size)
    queries = projected[:, :, 0:head_size]
    keys_own = projected[:, :, head_size : 2 * head_size].reshape(rows, heads_here * head_size)
    vals_own = projected[:, :, 2 * head_size : 3 * head_size].reshape(rows, heads_here * head_size)
    stacked = jnp.stack([keys_own, vals_own])
    near = from_behind(stacked, "song", 1)
    far = from_behind(stacked, "song", 2)
    every = jnp.concatenate([far, near, stacked], axis=1).reshape(
        2, 3 * rows, heads_here, head_size
    )
    all_keys = every[0]
    all_vals = every[1]
    scale = 1.0 / head_size**0.5
    key_rel = jnp.arange(3 * rows, dtype=jnp.int32) - 2 * rows
    lowest = -song_rank * rows
    span = min(rows, 512)
    outputs = []
    for begin in range(0, rows, span):
        q_blk = queries[begin : begin + span]
        scores = (
            jnp.einsum("qhd,khd->hqk", q_blk, all_keys, preferred_element_type=jnp.float32) * scale
        )
        query_pos = begin + jnp.arange(span, dtype=jnp.int32)
        valid = (key_rel[None, :] <= query_pos[:, None]) & (key_rel[None, :] >= lowest)
        scores = jnp.where(valid[None], scores, -1e30)
        top = jnp.max(scores, axis=-1, keepdims=True)
        expo = jnp.exp(scores - top)
        weights = (expo / jnp.sum(expo, axis=-1, keepdims=True)).astype(jnp.bfloat16)
        out = jnp.einsum("hqk,khd->qhd", weights, all_vals, preferred_element_type=jnp.float32)
        outputs.append(out.astype(jnp.bfloat16).reshape(span, heads_here * head_size))
    return jnp.concatenate(outputs, axis=0)


def solution(mesh):
    placed = (
        P("song"),
        P("song"),
        P(None, "tensor"),
        P(None, None, "tensor", None),
        P(None, None, "tensor"),
        P("tensor", None),
        P("tensor", None),
        P(),
        P(None, "tensor", None),
    )
    return jax.shard_map(
        on_device, mesh=mesh, in_specs=placed, out_specs=P("song", "tensor"), check_vma=False
    )
```

profile of v0, /device:TPU:3, one launch (start us, length us, event | category | flops | bytes accessed | tf_op | source)
XLA Modules:
  0.0 675.8 jit_solution(9196973381590233010)
XLA Ops:
  6.5 1.7 maximum_convert_fusion.12
  8.2 2.6 collective-permute-start.1
  10.8 3.4 collective-permute-start
  14.3 1.2 fusion.60
  16.2 1.2 fusion.58
  17.5 2.2 fusion.22
  19.7 68.5 %all-reduce.7 = bf16[256,1024]{1,0:T(8,128)(2,1)S(1)} all-reduce(f32[256,1024]{1,0:T(8,128)} %fusion.22), channel_id=1, replica_groups=mesh['song'=16,'tensor'=8] {'tensor'}, use_global_device_ids=true, to_apply=%region_0.0 | all-reduce | flops 262144 | bytes 1572864 | tf_op jit(solution)/shard_map/psum | solution.py:70
  88.2 1.9 maximum_convert_fusion.11
  90.1 17.1 %collective-permute-start.3 = (bf16[3,128]{1,0:T(4,128)(2,1)S(1)}, bf16[3,128]{1,0:T(4,128)(2,1)S(1)}, u32[]{:S(2)}, u32[]{:S(2)}) collective-permute-start(bf16[3,128]{1,0:T(4,128)(2,1)S(1)} %get-tuple-element.14), channel_id=1, source_target_pairs={{8,0},{16,8},{24,16},{32,24},{40,32},{48,40},{56,48},{64,56},{72,6... | collective-permute-start | bytes 2312 | tf_op jit(solution)/shard_map/ppermute | solution.py:19
  107.2 1.2 fusion.54
  108.4 1.9 collective-permute-start.2
  110.3 1.2 fusion.52
  111.6 1.2 fusion.21
  112.8 64.1 %all-reduce.8 = bf16[256,1024]{1,0:T(8,128)(2,1)S(1)} all-reduce(f32[256,1024]{1,0:T(8,128)S(1)} %fusion.21), channel_id=1, replica_groups=mesh['song'=16,'tensor'=8] {'tensor'}, use_global_device_ids=true, to_apply=%region_1.0 | all-reduce | flops 262144 | bytes 1572864 | tf_op jit(solution)/shard_map/psum | solution.py:70
  176.9 1.9 maximum_convert_fusion.10
  178.8 16.9 %collective-permute-start.5 = (bf16[9,128]{1,0:T(8,128)(2,1)S(1)}, bf16[9,128]{1,0:T(8,128)(2,1)S(1)}, u32[]{:S(2)}, u32[]{:S(2)}) collective-permute-start(bf16[9,128]{1,0:T(8,128)(2,1)S(1)} %get-tuple-element.12), channel_id=1, source_target_pairs={{8,0},{16,8},{24,16},{32,24},{40,32},{48,40},{56,48},{64,56},{72,6... | collective-permute-start | bytes 6920 | tf_op jit(solution)/shard_map/ppermute | solution.py:19
  195.8 1.2 fusion.48
  197.0 1.9 collective-permute-start.4
  198.9 1.2 fusion.46
  200.2 1.2 fusion.20
  201.4 67.9 %all-reduce.9 = bf16[256,1024]{1,0:T(8,128)(2,1)S(1)} all-reduce(f32[256,1024]{1,0:T(8,128)S(1)} %fusion.20), channel_id=1, replica_groups=mesh['song'=16,'tensor'=8] {'tensor'}, use_global_device_ids=true, to_apply=%region_2.0 | all-reduce | flops 262144 | bytes 1572864 | tf_op jit(solution)/shard_map/psum | solution.py:70
  269.3 1.9 maximum_convert_fusion.9
  271.2 17.1 %collective-permute-start.7 = (bf16[27,128]{1,0:T(8,128)(2,1)S(1)}, bf16[27,128]{1,0:T(8,128)(2,1)S(1)}, u32[]{:S(2)}, u32[]{:S(2)}) collective-permute-start(bf16[27,128]{1,0:T(8,128)(2,1)S(1)} %get-tuple-element.10), channel_id=1, source_target_pairs={{8,0},{16,8},{24,16},{32,24},{40,32},{48,40},{56,48},{64,56},{72,6... | collective-permute-start | bytes 20744 | tf_op jit(solution)/shard_map/ppermute | solution.py:19
  288.3 1.2 fusion.42
  289.6 1.9 collective-permute-start.6
  291.5 1.2 fusion.40
  292.7 1.2 fusion.19
  294.0 64.3 %all-reduce.10 = bf16[256,1024]{1,0:T(8,128)(2,1)S(1)} all-reduce(f32[256,1024]{1,0:T(8,128)S(1)} %fusion.19), channel_id=1, replica_groups=mesh['song'=16,'tensor'=8] {'tensor'}, use_global_device_ids=true, to_apply=%region_3.0 | all-reduce | flops 262144 | bytes 1572864 | tf_op jit(solution)/shard_map/psum | solution.py:70
  358.3 5.5 fusion.30
  363.7 9.2 %reshape.128 = f32[1024,1920]{1,0:T(8,128)} reshape(f32[256,7680]{1,0:T(8,128)} %fusion.30) | data formatting | bytes 15728640 | tf_op jit(solution)/shard_map/reshape | solution.py:75
  373.0 7.7 %convolution_add_fusion = f32[1024,1920]{1,0:T(8,128)} fusion(f32[1024,1920]{1,0:T(8,128)} %reshape.128, bf16[256,1920]{1,0:T(8,128)(2,1)S(1)} %copy-done.6, s32[1024]{0:T(1024)S(1)} %broadcast_subtract_fusion), kind=kOutput, calls=%fused_computation.23 | convolution fusion | flops 1008861184 | bytes 16715776 | tf_op jit(solution)/shard_map/dot_general | solution.py:82
  380.7 4.0 copy.24
  384.7 184.2 %all-reduce.6.cloned.1.call-done = f32[1024,1920]{1,0:T(8,128)} async-done(((f32[1024,1920]{1,0:T(8,128)}), f32[1024,1920]{1,0:T(8,128)}) %all-reduce.6.cloned.1.call-update) | async-done | bytes 7864336 | tf_op jit(solution)/shard_map/psum | solution.py:83
  568.9 3.7 reduce_sum.36
  572.6 4.3 multiply_reduce_fusion
  578.0 5.8 fusion.18
  583.8 1.2 copy-done.7
  586.2 3.7 collective-permute-start.9
  589.9 3.2 collective-permute-start.8
  593.1 3.3 fusion.8
  596.4 14.2 %collective-permute-done.9 = bf16[2,1024,256]{1,2,0:T(8,128)(2,1)} collective-permute-done((bf16[2,1024,256]{1,2,0:T(8,128)(2,1)}, bf16[2,1024,256]{1,2,0:T(8,128)(2,1)}, u32[]{:S(2)}, u32[]{:S(2)}) %collective-permute-start.9) | collective-permute-done | bytes 1048608 | tf_op jit(solution)/shard_map/ppermute | solution.py:29
  610.6 16.5 %collective-permute-done.8 = bf16[2,1024,256]{1,2,0:T(8,128)(2,1)} collective-permute-done((bf16[2,1024,256]{1,2,0:T(8,128)(2,1)}, bf16[2,1024,256]{1,2,0:T(8,128)(2,1)}, u32[]{:S(2)}, u32[]{:S(2)}) %collective-permute-start.8) | collective-permute-done | bytes 1048608 | tf_op jit(solution)/shard_map/ppermute | solution.py:29
  627.2 1.9 maximum_maximum_fusion
  629.1 1.8 fusion.119
  631.1 10.8 %fusion.125 = (f32[2,512]{1,0:T(2,128)S(1)}, f32[2,512,3072]{2,1,0:T(8,128)}) fusion(pred[512,3072]{1,0:T(8,128)(4,1)S(1)} %copy-done.3, bf16[3072,2,128]{0,2,1:T(8,128)(2,1)} %bitcast.90, bf16[1024,2,384]{0,2,1:T(8,128)(2,1)} %bitcast.93), kind=kOutput, calls=%fused_computation.157 | convolution fusion | flops 817892352 | bytes 15994880 | tf_op jit(solution)/shard_map/sub | solution.py:120
  641.9 7.5 %fusion.27 = bf16[2,128,512]{2,1,0:T(8,128)(2,1)S(1)} fusion(bf16[3072,2,128]{0,2,1:T(8,128)(2,1)} %bitcast.88, f32[2,512,3072]{2,1,0:T(8,128)} %get-tuple-element.28, f32[2,512]{1,0:T(2,128)S(1)} %get-tuple-element.27), kind=kOutput, calls=%fused_computation.42 | convolution fusion | flops 811728896 | bytes 14422016 | tf_op jit(solution)/shard_map/hqk,khd->qhd/dot_general | solution.py:122
  650.2 10.3 %fusion.130 = (f32[2,512]{1,0:T(2,128)S(1)}, f32[2,512,3072]{2,1,0:T(8,128)}) fusion(pred[512,3072]{1,0:T(8,128)(4,1)S(1)} %get-tuple-element.17, bf16[3072,2,128]{0,2,1:T(8,128)(2,1)S(1)} %bitcast.91, bf16[1024,2,384]{0,2,1:T(8,128)(2,1)} %bitcast.94), kind=kOutput, calls=%fused_computation.158 | convolution fusion | flops 817892352 | bytes 15994880 | tf_op jit(solution)/shard_map/sub | solution.py:120
  660.5 7.5 %fusion.28 = bf16[2,128,512]{2,1,0:T(8,128)(2,1)S(1)} fusion(bf16[3072,2,128]{0,2,1:T(8,128)(2,1)} %bitcast.89, f32[2,512,3072]{2,1,0:T(8,128)} %get-tuple-element.30, f32[2,512]{1,0:T(2,128)S(1)} %get-tuple-element.29), kind=kOutput, calls=%fused_computation.43 | convolution fusion | flops 811728896 | bytes 14422016 | tf_op jit(solution)/shard_map/hqk,khd->qhd/dot_general | solution.py:122
  (42 shorter events, 5.1 us)
Async XLA Ops:
  6.5 351.7 %copy-start = (bf16[128,7680]{1,0:T(8,128)(2,1)S(1)}, bf16[128,7680]{1,0:T(8,128)(2,1)}, u32[]{:S(2)}) copy-start(bf16[128,7680]{1,0:T(8,128)(2,1)} %param.14) | copy-start | bytes 5898244
  6.5 562.4 %all-reduce.6.cloned.1.call-start = ((), (), s32[]{:S(2)}) async-start(), calls=%async_computation | async-start | bytes 15728640 | tf_op jit(solution)/shard_map/psum | solution.py:83
  8.2 8.0 %collective-permute-start.1 = (bf16[1,128]{1,0:T(2,128)(2,1)S(1)}, bf16[1,128]{1,0:T(2,128)(2,1)S(1)}, u32[]{:S(2)}, u32[]{:S(2)}) collective-permute-start(bf16[1,128]{1,0:T(2,128)(2,1)S(1)} %get-tuple-element.16), channel_id=1, source_target_pairs={{8,0},{16,8},{24,16},{32,24},{40,32},{48,40},{56,48},{64,56},{72,6... | collective-permute-start | bytes 776 | tf_op jit(solution)/shard_map/ppermute | solution.py:19
  10.8 6.6 collective-permute-start
  90.1 20.2 %collective-permute-start.3 = (bf16[3,128]{1,0:T(4,128)(2,1)S(1)}, bf16[3,128]{1,0:T(4,128)(2,1)S(1)}, u32[]{:S(2)}, u32[]{:S(2)}) collective-permute-start(bf16[3,128]{1,0:T(4,128)(2,1)S(1)} %get-tuple-element.14), channel_id=1, source_target_pairs={{8,0},{16,8},{24,16},{32,24},{40,32},{48,40},{56,48},{64,56},{72,6... | collective-permute-start | bytes 2312 | tf_op jit(solution)/shard_map/ppermute | solution.py:19
  108.4 3.2 collective-permute-start.2
  178.8 20.1 %collective-permute-start.5 = (bf16[9,128]{1,0:T(8,128)(2,1)S(1)}, bf16[9,128]{1,0:T(8,128)(2,1)S(1)}, u32[]{:S(2)}, u32[]{:S(2)}) collective-permute-start(bf16[9,128]{1,0:T(8,128)(2,1)S(1)} %get-tuple-element.12), channel_id=1, source_target_pairs={{8,0},{16,8},{24,16},{32,24},{40,32},{48,40},{56,48},{64,56},{72,6... | collective-permute-start | bytes 6920 | tf_op jit(solution)/shard_map/ppermute | solution.py:19
  197.0 3.2 collective-permute-start.4
  271.2 20.3 %collective-permute-start.7 = (bf16[27,128]{1,0:T(8,128)(2,1)S(1)}, bf16[27,128]{1,0:T(8,128)(2,1)S(1)}, u32[]{:S(2)}, u32[]{:S(2)}) collective-permute-start(bf16[27,128]{1,0:T(8,128)(2,1)S(1)} %get-tuple-element.10), channel_id=1, source_target_pairs={{8,0},{16,8},{24,16},{32,24},{40,32},{48,40},{56,48},{64,56},{72,6... | collective-permute-start | bytes 20744 | tf_op jit(solution)/shard_map/ppermute | solution.py:19
  289.6 3.2 collective-permute-start.6
  363.7 9.3 %copy-start.6 = (bf16[256,1920]{1,0:T(8,128)(2,1)S(1)}, bf16[256,1920]{1,0:T(8,128)(2,1)}, u32[]{:S(2)}) copy-start(bf16[256,1920]{1,0:T(8,128)(2,1)} %param.15) | copy-start | bytes 2949124
  572.6 5.5 copy-start.2
  572.6 5.5 copy-start.8
  583.8 1.2 copy-start.7
  586.2 24.5 %collective-permute-start.9 = (bf16[2,1024,256]{1,2,0:T(8,128)(2,1)}, bf16[2,1024,256]{1,2,0:T(8,128)(2,1)}, u32[]{:S(2)}, u32[]{:S(2)}) collective-permute-start(bf16[2,1024,256]{1,2,0:T(8,128)(2,1)} %pad_maximum_fusion), channel_id=1, source_target_pairs={{0,8},{8,16},{16,24},{24,32},{32,40},{40,48},{48,56},{56,64},{64,7... | collective-permute-start | bytes 3145736 | tf_op jit(solution)/shard_map/ppermute | solution.py:29
  589.9 37.2 %collective-permute-start.8 = (bf16[2,1024,256]{1,2,0:T(8,128)(2,1)}, bf16[2,1024,256]{1,2,0:T(8,128)(2,1)}, u32[]{:S(2)}, u32[]{:S(2)}) collective-permute-start(bf16[2,1024,256]{1,2,0:T(8,128)(2,1)} %pad_maximum_fusion), channel_id=1, source_target_pairs={{0,16},{8,24},{16,32},{24,40},{32,48},{40,56},{48,64},{56,72},{64,... | collective-permute-start | bytes 3145736 | tf_op jit(solution)/shard_map/ppermute | solution.py:29
  629.1 2.0 copy-start.3
  641.9 8.3 %copy-start.4 = (bf16[1,3072,256]{1,2,0:T(8,128)(2,1)S(1)}, bf16[1,3072,256]{1,2,0:T(8,128)(2,1)}, u32[]{:S(2)}) copy-start(bf16[1,3072,256]{1,2,0:T(8,128)(2,1)} %get-tuple-element.5) | copy-start | bytes 4718596
  660.5 7.6 %copy-start.5 = (bf16[512,256]{1,0:T(8,128)(2,1)S(1)}, bf16[512,256]{1,0:T(8,128)(2,1)}, u32[]{:S(2)}) copy-start(bf16[512,256]{1,0:T(8,128)(2,1)} %copy.19) | copy-start | bytes 786436
  660.5 8.5 %copy-start.1 = (bf16[128,7680]{1,0:T(8,128)(2,1)S(1)}, bf16[128,7680]{1,0:T(8,128)(2,1)}, u32[]{:S(2)}) copy-start(bf16[128,7680]{1,0:T(8,128)(2,1)} %param.14) | copy-start | bytes 5898244
Sparse Core Ops, SparseCore 0:
  380.8 188.0 all-reduce.5
where the time goes:
time: 677 us; the launch traced here: 676 us
  blocking collectives  265 us (39%)
  waiting for transfers between devices  215 us (32%)
  matrix products  78.2 us (12%)
  starting transfers between devices  69.8 us (10%)
  local copies, waits for them, and re-layouts  18.7 us (3%)
  other arithmetic  15.7 us (2%)
  between operations  13.8 us (2%)
    psum x4, blocking collectives, on_device(): summed = lax.psum(partial_value, 'tensor')  265 us
    psum x1, waiting for transfers between devices, on_device(): frames = lax.psum(terms, 'tensor')  184 us
    ppermute x4, starting transfers between devices, extended(): lax.ppermute(head, axis, [((i + 1) % count, i) for i in range(ends)])  53.6 us
    ppermute x2, waiting for transfers between devices, from_behind(): return lax.ppermute(shard, axis, pairs)  30.8 us
    sub x2, matrix products, on_device(): expo = jnp.exp(scores - top)  21.1 us
    dot_general x2, matrix products, on_device(): jnp.einsum('hqk,khd->qhd', weights, all_vals, preferred_element_type=jnp....  15 us
  transfers between devices with their start and end apart: 11, of which 3 were waited for; matrix products, arithmetic and copies ran while one was open for 3% of the time, Pallas kernels for 0%

commit v1 on v0

--- a/solution.py
+++ b/solution.py
@@ -67,7 +67,8 @@
             dilated_weight[level, 2],
             preferred_element_type=jnp.float32,
         )
-        summed = lax.psum(partial_value, "tensor")
+        shards = lax.all_gather(partial_value, "tensor")
+        summed = jnp.sum(shards, axis=0)
         rect = jnp.maximum(summed, 0.0).astype(jnp.bfloat16)
         state = state + jnp.dot(rect, mixing_weight[level], preferred_element_type=jnp.float32)
     final = state.astype(jnp.bfloat16)

time: 677 us -> 808 us (1.19)
  waiting for transfers between devices: 215 us -> 629 us
  blocking collectives: 265 us -> 0 us
  starting transfers between devices: 69.8 us -> 31.5 us
  other arithmetic: 15.7 us -> 32.7 us
    all_gather x0 -> x4, waiting for transfers between devices: none -> 425 us  [on_device(): shards = lax.all_gather(partial_value, 'tensor')]
    psum x4 -> x0, blocking collectives: 265 us -> none  [on_device(): summed = lax.psum(partial_value, 'tensor')]
    ppermute x4, starting transfers between devices: 53.6 us -> 11.5 us  [extended(): lax.ppermute(head, axis, [((i + 1) % count, i) for i in range(ends)])]
    reduce_sum x0 -> x4, other arithmetic: none -> 17.6 us  [on_device(): summed = jnp.sum(shards, axis=0)]
    psum x1, waiting for transfers between devices: 184 us -> 170 us  [on_device(): frames = lax.psum(terms, 'tensor')]
  transfers between devices with their start and end apart: 11 -> 15, of which waited for: 3 -> 10; matrix products, arithmetic and copies ran while one was open for 3% -> 2% of each run, Pallas kernels for 0% -> 0%
where the time goes in v1:
time: 808 us; the launch traced here: 807 us
  waiting for transfers between devices  629 us (78%)
  matrix products  81.2 us (10%)
  other arithmetic  32.7 us (4%)
  starting transfers between devices  31.5 us (4%)
  local copies, waits for them, and re-layouts  18.7 us (2%)
  between operations  13.5 us (2%)
    all_gather x4, waiting for transfers between devices, on_device(): shards = lax.all_gather(partial_value, 'tensor')  425 us
    psum x1, waiting for transfers between devices, on_device(): frames = lax.psum(terms, 'tensor')  170 us
    ppermute x2, waiting for transfers between devices, from_behind(): return lax.ppermute(shard, axis, pairs)  30.7 us
    sub x2, matrix products, on_device(): expo = jnp.exp(scores - top)  21 us
    reduce_sum x4, other arithmetic, on_device(): summed = jnp.sum(shards, axis=0)  17.6 us
  transfers between devices with their start and end apart: 15, of which 10 were waited for; matrix products, arithmetic and copies ran while one was open for 2% of the time, Pallas kernels for 0%

profile of v1, /device:TPU:3, one launch (start us, length us, event | category | flops | bytes accessed | tf_op | source)
XLA Modules:
  0.0 806.7 jit_solution(6649281607524657382)
XLA Ops:
  6.5 2.3 maximum_convert_fusion.12
  8.9 2.6 collective-permute-start.1
  11.5 3.4 collective-permute-start
  14.9 1.2 fusion.60
  16.2 1.2 fusion.58
  17.4 2.3 fusion.22
  19.8 109.2 %all-gather.9.cloned.1.call-done = f32[2048,1024]{1,0:T(8,128)} async-done(((f32[256,1024]{1,0:T(8,128)}), f32[2048,1024]{1,0:T(8,128)}) %all-gather.9.cloned.1.call-update) | async-done | bytes 8388624 | tf_op jit(solution)/shard_map/all_gather | solution.py:70
  129.0 4.5 reduce_sum.72
  133.5 1.9 maximum_convert_fusion.11
  135.4 3.0 collective-permute-start.3
  138.4 1.2 fusion.54
  139.6 3.1 collective-permute-start.2
  145.0 2.3 fusion.21
  147.4 105.2 %all-gather.11.cloned.1.call-done = f32[2048,1024]{1,0:T(8,128)} async-done(((f32[256,1024]{1,0:T(8,128)}), f32[2048,1024]{1,0:T(8,128)}) %all-gather.11.cloned.1.call-update) | async-done | bytes 8388624 | tf_op jit(solution)/shard_map/all_gather | solution.py:70
  252.6 4.4 reduce_sum.73
  256.9 1.9 maximum_convert_fusion.10
  258.8 3.0 collective-permute-start.5
  261.8 1.2 fusion.48
  263.0 3.1 collective-permute-start.4
  268.4 2.3 fusion.20
  270.8 105.2 %all-gather.13.cloned.1.call-done = f32[2048,1024]{1,0:T(8,128)} async-done(((f32[256,1024]{1,0:T(8,128)}), f32[2048,1024]{1,0:T(8,128)}) %all-gather.13.cloned.1.call-update) | async-done | bytes 8388624 | tf_op jit(solution)/shard_map/all_gather | solution.py:70
  376.0 4.4 reduce_sum.74
  380.4 1.2 maximum_convert_fusion.9
  381.7 3.0 collective-permute-start.7
  385.9 3.1 collective-permute-start.6
  389.0 1.2 fusion.40
  391.4 2.3 fusion.19
  393.9 105.0 %all-gather.15.cloned.1.call-done = f32[2048,1024]{1,0:T(8,128)} async-done(((f32[256,1024]{1,0:T(8,128)}), f32[2048,1024]{1,0:T(8,128)}) %all-gather.15.cloned.1.call-update) | async-done | bytes 8388624 | tf_op jit(solution)/shard_map/all_gather | solution.py:70
  499.0 4.4 reduce_sum.75
  503.4 5.4 fusion.30
  508.8 9.2 %reshape.128 = f32[1024,1920]{1,0:T(8,128)} reshape(f32[256,7680]{1,0:T(8,128)} %fusion.30) | data formatting | bytes 15728640 | tf_op jit(solution)/shard_map/reshape | solution.py:76
  518.0 7.7 convolution_add_fusion
  525.7 4.0 copy.24
  529.8 170.4 %all-reduce.2.cloned.1.call-done = f32[1024,1920]{1,0:T(8,128)} async-done(((f32[1024,1920]{1,0:T(8,128)}), f32[1024,1920]{1,0:T(8,128)}) %all-reduce.2.cloned.1.call-update) | async-done | bytes 7864336 | tf_op jit(solution)/shard_map/psum | solution.py:84
  700.2 3.7 reduce_sum.76
  703.8 4.3 multiply_reduce_fusion
  709.3 5.8 fusion.18
  717.4 3.7 collective-permute-start.9
  721.2 3.2 collective-permute-start.8
  724.4 3.3 fusion.8
  727.7 14.2 %collective-permute-done.9 = bf16[2,1024,256]{1,2,0:T(8,128)(2,1)} collective-permute-done((bf16[2,1024,256]{1,2,0:T(8,128)(2,1)}, bf16[2,1024,256]{1,2,0:T(8,128)(2,1)}, u32[]{:S(2)}, u32[]{:S(2)}) %collective-permute-start.9) | collective-permute-done | bytes 1048608 | tf_op jit(solution)/shard_map/ppermute | solution.py:29
  741.9 16.5 %collective-permute-done.8 = bf16[2,1024,256]{1,2,0:T(8,128)(2,1)} collective-permute-done((bf16[2,1024,256]{1,2,0:T(8,128)(2,1)}, bf16[2,1024,256]{1,2,0:T(8,128)(2,1)}, u32[]{:S(2)}, u32[]{:S(2)}) %collective-permute-start.8) | collective-permute-done | bytes 1048608 | tf_op jit(solution)/shard_map/ppermute | solution.py:29
  758.4 1.9 maximum_maximum_fusion
  760.3 1.8 fusion.119
  762.4 10.8 %fusion.125 = (f32[2,512]{1,0:T(2,128)S(1)}, f32[2,512,3072]{2,1,0:T(8,128)}) fusion(pred[512,3072]{1,0:T(8,128)(4,1)S(1)} %copy-done.3, bf16[3072,2,128]{0,2,1:T(8,128)(2,1)} %bitcast.98, bf16[1024,2,384]{0,2,1:T(8,128)(2,1)} %bitcast.101), kind=kOutput, calls=%fused_computation.157 | convolution fusion | flops 817892352 | bytes 15994880 | tf_op jit(solution)/shard_map/sub | solution.py:121
  773.1 7.5 fusion.27
  781.5 10.2 %fusion.130 = (f32[2,512]{1,0:T(2,128)S(1)}, f32[2,512,3072]{2,1,0:T(8,128)}) fusion(pred[512,3072]{1,0:T(8,128)(4,1)S(1)} %get-tuple-element.17, bf16[3072,2,128]{0,2,1:T(8,128)(2,1)S(1)} %bitcast.99, bf16[1024,2,384]{0,2,1:T(8,128)(2,1)} %bitcast.102), kind=kOutput, calls=%fused_computation.158 | convolution fusion | flops 817892352 | bytes 15994880 | tf_op jit(solution)/shard_map/sub | solution.py:121
  791.7 7.5 fusion.28
  (60 shorter events, 13.0 us)
Async XLA Ops:
  6.5 496.8 %copy-start = (bf16[128,7680]{1,0:T(8,128)(2,1)S(1)}, bf16[128,7680]{1,0:T(8,128)(2,1)}, u32[]{:S(2)}) copy-start(bf16[128,7680]{1,0:T(8,128)(2,1)} %param.14) | copy-start | bytes 5898244
  6.5 122.5 %all-gather.9.cloned.1.call-start = ((), (), s32[]{:S(2)}) async-start(), calls=%async_computation.1 | async-start | bytes 9437184 | tf_op jit(solution)/shard_map/all_gather | solution.py:70
  8.9 7.3 collective-permute-start.1
  11.5 6.0 collective-permute-start
  19.7 232.8 %all-gather.11.cloned.1.call-start = ((), (), s32[]{:S(2)}) async-start(), calls=%async_computation.2 | async-start | bytes 9437184 | tf_op jit(solution)/shard_map/all_gather | solution.py:70
  129.0 4.5 copy-start.8
  135.4 7.3 collective-permute-start.3
  139.6 5.4 collective-permute-start.2
  147.3 228.7 %all-gather.13.cloned.1.call-start = ((), (), s32[]{:S(2)}) async-start(), calls=%async_computation.3 | async-start | bytes 9437184 | tf_op jit(solution)/shard_map/all_gather | solution.py:70
  258.8 7.3 collective-permute-start.5
  263.0 5.4 collective-permute-start.4
  270.8 228.2 %all-gather.15.cloned.1.call-start = ((), (), s32[]{:S(2)}) async-start(), calls=%async_computation.4 | async-start | bytes 9437184 | tf_op jit(solution)/shard_map/all_gather | solution.py:70
  376.0 4.4 copy-start.11
  381.7 7.3 collective-permute-start.7
  385.9 8.0 copy-start.9
  385.9 5.4 collective-permute-start.6
  393.7 306.5 %all-reduce.2.cloned.1.call-start = ((), (), s32[]{:S(2)}) async-start(), calls=%async_computation | async-start | bytes 15728640 | tf_op jit(solution)/shard_map/psum | solution.py:84
  508.8 9.3 %copy-start.6 = (bf16[256,1920]{1,0:T(8,128)(2,1)S(1)}, bf16[256,1920]{1,0:T(8,128)(2,1)}, u32[]{:S(2)}) copy-start(bf16[256,1920]{1,0:T(8,128)(2,1)} %param.15) | copy-start | bytes 2949124
  703.8 5.5 copy-start.2
  703.8 5.5 copy-start.10
  715.1 1.2 copy-start.7
  717.4 24.5 %collective-permute-start.9 = (bf16[2,1024,256]{1,2,0:T(8,128)(2,1)}, bf16[2,1024,256]{1,2,0:T(8,128)(2,1)}, u32[]{:S(2)}, u32[]{:S(2)}) collective-permute-start(bf16[2,1024,256]{1,2,0:T(8,128)(2,1)} %pad_maximum_fusion), channel_id=1, source_target_pairs={{0,8},{8,16},{16,24},{24,32},{32,40},{40,48},{48,56},{56,64},{64,7... | collective-permute-start | bytes 3145736 | tf_op jit(solution)/shard_map/ppermute | solution.py:29
  721.2 37.2 %collective-permute-start.8 = (bf16[2,1024,256]{1,2,0:T(8,128)(2,1)}, bf16[2,1024,256]{1,2,0:T(8,128)(2,1)}, u32[]{:S(2)}, u32[]{:S(2)}) collective-permute-start(bf16[2,1024,256]{1,2,0:T(8,128)(2,1)} %pad_maximum_fusion), channel_id=1, source_target_pairs={{0,16},{8,24},{16,32},{24,40},{32,48},{40,56},{48,64},{56,72},{64,... | collective-permute-start | bytes 3145736 | tf_op jit(solution)/shard_map/ppermute | solution.py:29
  760.3 2.0 copy-start.3
  773.1 8.3 %copy-start.4 = (bf16[1,3072,256]{1,2,0:T(8,128)(2,1)S(1)}, bf16[1,3072,256]{1,2,0:T(8,128)(2,1)}, u32[]{:S(2)}) copy-start(bf16[1,3072,256]{1,2,0:T(8,128)(2,1)} %get-tuple-element.5) | copy-start | bytes 4718596
  791.7 7.6 copy-start.5
  791.7 8.5 %copy-start.1 = (bf16[128,7680]{1,0:T(8,128)(2,1)S(1)}, bf16[128,7680]{1,0:T(8,128)(2,1)}, u32[]{:S(2)}) copy-start(bf16[128,7680]{1,0:T(8,128)(2,1)} %param.14) | copy-start | bytes 5898244
Sparse Core Ops, SparseCore 0:
  19.9 109.1 all-gather.8
  147.4 105.0 all-gather.10
  270.9 105.0 all-gather.12
  393.8 105.1 all-gather.14
  525.8 174.2 all-reduce.1
